TPU v7x, 32 devices: a whole 2x2x4 slice. The times are simulated.
32 devices in a mesh: cls: 8 (over z, x), img: 4 (over y, core).
Axes of the slice: x: 2, y: 2, z: 4, core: 2. Of those that a mesh axis runs over, the one named last changes fastest.
Arguments:
- images: bfloat16 [512, 9216], P(('cls', 'img')), may hold values from -9 to 9
- ctf: bfloat16 [512, 4608], P(('cls', 'img')), may hold values from -1 to 1
- classes: int32 [512, 4], P(('cls', 'img')), may hold values from 0 to 55, as said below
- class_place: int32 [56], replicated, may hold values from 0 to 55, as said below
- references: bfloat16 [56, 9216], P('cls'), may hold values from -3 to 3
- sigma2: float32 [64], replicated, may hold values from 0.05 to 4, as said below
Outputs:
- new_references: float32 [56, 9216], P('cls', 'img')
Inputs may be any that keep to these rules, and one draw needn't show every extreme that they name: Each particle names 4 different classes whose table rows class_place[k] lie in 4 different groups of 7 consecutive table rows. Among the 16 particles of one device (aligned blocks of 16 rows) at most 8 list entries fall in one group, and in every block some group receives exactly 8. A permutation: class k is held in table row class_place[k]. `sigma2`: positive noise powers.
All inputs are finite; a program needn't handle non-finite values.
Results may differ from a plain program's by a relative error of at most 0.0018.
Values may be sent and summed in bfloat16 or wider, within the bound.
A program may use at most 128 MiB of HBM per device.

v0:
```python
import functools

import jax
import jax.numpy as jnp
from jax import lax
from jax.experimental import pallas as pl
from jax.experimental.pallas import tpu as pltpu
from jax.sharding import PartitionSpec as P

MESH = pl.DeviceIdType.MESH
VMEM = pltpu.VMEM
F32 = jnp.float32
BF16 = jnp.bfloat16
LANES = 128


def vmem_specs(count):
    return [pl.BlockSpec(memory_space=pltpu.VMEM)] * count


def greet(groups):
    barrier = pltpu.get_barrier_semaphore()
    total = 0
    for axis, size in groups:
        me = lax.axis_index(axis)
        for step in range(1, size):
            peer = lax.rem(me + step, size)
            pl.semaphore_signal(barrier, inc=1, device_id={axis: peer}, device_id_type=MESH)
            total += 1
    pl.semaphore_wait(barrier, total)


def lane_of(shape):
    return lax.broadcasted_iota(jnp.int32, shape, len(shape) - 1)


def roll(x, shift):
    return pltpu.roll(x, shift % LANES, x.ndim - 1)


def score_kernel(
    dims, place_ref, w_ref, r_ref, t_ref, sigma_ref, parts, weights_ref, tall, wall, rall, rows_ref,
    table, low, high, pick_num, pick_den,
    own_sem, ws, wr, rs, rr, ts, tr, ls, lr,
):
    fellows, particles, owners, per_owner, slots, top, angles, half = dims
    width = 2 * half
    per_pack = LANES // width
    per_den = LANES // half
    tall_rows = table.shape[1]
    num_packs = particles // per_pack
    tiles = angles // 8
    cut = (tiles // 2 + tiles % 2) * 8
    my_owner = lax.axis_index("cls")
    my_fellow = lax.axis_index("img")
    greet((("cls", owners), ("img", fellows)))

    def remote(src, dst, send, recv, axis, peer):
        return pltpu.make_async_remote_copy(
            src_ref=src,
            dst_ref=dst,
            send_sem=send,
            recv_sem=recv,
            device_id={axis: peer},
            device_id_type=MESH,
        )

    row_copies = []
    ref_copies = []
    image_copies = []
    for step in range(1, fellows):
        peer = lax.rem(my_fellow + step, fellows)
        row_copies.append(remote(t_ref, tall.at[my_fellow], ts.at[step], tr.at[step], "img", peer))
        image_copies.append(
            remote(w_ref.at[peer], wall.at[my_fellow], ws.at[step], wr.at[step], "img", peer)
        )
    for step in range(1, owners):
        peer = lax.rem(my_owner + step, owners)
        ref_copies.append(remote(r_ref, rall.at[my_owner], rs.at[step], rr.at[step], "cls", peer))
    for copy in row_copies + ref_copies + image_copies:
        copy.start()
    own_rows = pltpu.make_async_copy(t_ref, tall.at[my_fellow], own_sem.at[0])
    own_rows.start()

    lane = lane_of((angles, LANES))
    zero_tail = jnp.zeros((LANES - angles, LANES), F32)
    source_lane = lax.broadcasted_iota(jnp.int32, (LANES, LANES), 0)
    target_lane = lax.broadcasted_iota(jnp.int32, (LANES, LANES), 1)
    shell = target_lane % half
    num_source = jnp.where(target_lane < width, 2 * shell + target_lane // half, -LANES)
    for g in range(per_pack):
        pick_num[g] = (source_lane == num_source + width * g).astype(F32).astype(BF16)
    den_source = jnp.where(target_lane < width + half, shell, -LANES)
    for g in range(per_den):
        pick_den[g] = (source_lane == den_source + half * g).astype(F32).astype(BF16)
    spread = jnp.concatenate([1.0 / sigma_ref[...]] * (LANES // sigma_ref.shape[1]), axis=1)
    spread = jnp.broadcast_to(spread, (8, LANES))
    row_lane = lane_of((8, LANES))
    inverse = jnp.zeros((8, LANES), F32)
    for part in range(3):
        shift = lax.rem(half * part - half * my_fellow + LANES, LANES)
        inverse = jnp.where(row_lane // half == part, pltpu.roll(spread, shift, 1), inverse)
    inverse = inverse[0:1]

    def place(fellow, read):
        def some(u, carry):
            for g in range(per_den):
                num = jnp.dot(
                    read(u * (per_den // per_pack) + g // per_pack),
                    pick_num[g % per_pack],
                    preferred_element_type=F32,
                )
                den = jnp.dot(read(num_packs + u), pick_den[g], preferred_element_type=F32)
                joined = jnp.where(lane < width, num, den) * (den * inverse)
                weights_ref[fellow * particles + u * per_den + g] = jnp.concatenate(
                    [joined, zero_tail], axis=0
                ).astype(BF16)
            return carry

        lax.fori_loop(0, particles // per_den, some, 0)

    def tabulate(owner, read):
        for t in range(per_owner):
            ref = jnp.dot(read(t // per_pack), pick_num[t % per_pack], preferred_element_type=F32)
            square = ref * ref
            power = (square + roll(square, -half)).astype(BF16).astype(F32) * -0.5
            power = roll(power, width)
            joined = jnp.where(lane < width, ref, jnp.where(lane < width + half, power, 0.0))
            table[owner * per_owner + t] = jnp.concatenate(
                [joined, jnp.zeros((tall_rows - angles, LANES), F32)], axis=0
            ).astype(BF16)

    place(my_fellow, lambda u: w_ref[my_fellow, u])
    tabulate(my_owner, lambda u: r_ref[u])
    own_rows.wait()
    for copy in row_copies:
        copy.wait_recv()
    to_smem = pltpu.make_async_copy(tall, rows_ref, own_sem.at[1])
    to_smem.start()
    for step in range(1, max(owners, fellows)):
        if step < fellows:
            image_copies[step - 1].wait_recv()
            source = lax.rem(my_fellow + fellows - step, fellows)
            place(source, lambda u: wall[source, u])
        if step < owners:
            ref_copies[step - 1].wait_recv()
            holder = lax.rem(my_owner + owners - step, owners)
            tabulate(holder, lambda u: rall[holder, u])
    to_smem.wait()

    batch = 8

    def score(fellow, begin):
        lows = []
        highs = []
        for k in range(batch):
            i = begin + k
            refs = jnp.concatenate([table[place_ref[rows_ref[fellow, i, j]]] for j in range(top)], axis=0)
            grid = lax.dot_general(
                refs,
                weights_ref[fellow * particles + i],
                (((1,), (1,)), ((), ())),
                preferred_element_type=F32,
            )
            for j in range(top):
                base = j * tall_rows
                lo = grid[base : base + 8]
                for tile in range(1, cut // 8):
                    lo = lo + roll(grid[base + 8 * tile : base + 8 * tile + 8], 8 * tile)
                hi = grid[base + cut : base + cut + 8]
                for tile in range(cut // 8 + 1, tiles):
                    hi = hi + roll(grid[base + 8 * tile : base + 8 * tile + 8], 8 * tile - cut)
                lo = pltpu.roll(lo, 0, 1, stride=1, stride_axis=0)
                hi = pltpu.roll(hi, 0, 1, stride=1, stride_axis=0)
                lows.append(jnp.sum(lo, axis=0, keepdims=True))
                highs.append(jnp.sum(hi, axis=0, keepdims=True))
        rows = batch * top
        start = pl.multiple_of(begin * top, rows)
        low[pl.ds(start, rows)] = jnp.concatenate(lows, axis=0)
        high[pl.ds(start, rows)] = jnp.concatenate(highs, axis=0)

    part_copies = []
    chunk = particles * top
    for fellow in range(fellows):

        def some(b, carry):
            score(fellow, b * batch)
            return carry

        lax.fori_loop(0, particles // batch, some, 0)
        lo = low[...]
        hi = high[...]
        spot = lane_of(lo.shape)
        total = roll(lo, 1) + jnp.where(spot < cut, roll(lo, 1 - angles), 0.0)
        back = angles - 1 - cut
        total = total + roll(hi, -back) + jnp.where(spot >= cut + 1, roll(hi, cut + 1), 0.0)
        place_at = parts.at[my_fellow, pl.ds(fellow * chunk, chunk)]
        parts[my_fellow, pl.ds(fellow * chunk, chunk)] = jnp.where(spot < angles, total, 0.0)
        for step in range(1, fellows):
            peer = lax.rem(my_fellow + step, fellows)
            copy = remote(place_at, place_at, ls.at[step, fellow], lr.at[step, fellow], "img", peer)
            copy.start()
            part_copies.append(copy)
    for copy in row_copies + ref_copies + image_copies:
        copy.wait_send()
    for copy in part_copies:
        copy.wait()


def group_of(x, top, combine):
    row = lax.broadcasted_iota(jnp.int32, x.shape, 0)
    count = x.shape[0]
    step = 1
    while step < top:
        swapped = jnp.where(
            (row // step) % 2 == 0, pltpu.roll(x, count - step, 0), pltpu.roll(x, step, 0)
        )
        x = combine(x, swapped)
        step *= 2
    return x


def total_kernel(dims, place_ref, rows_ref, parts, weights_ref, out_ref, acc, ext_lo, ext_hi):
    fellows, particles, owners, per_owner, slots, top, angles, half = dims
    width = 2 * half
    per_pack = LANES // width
    per_den = LANES // half
    num_packs = slots // per_pack
    cut = (angles // 16) * 8 + (8 if (angles // 8) % 2 else 0)
    tiles = angles // 8
    tall_rows = -(-angles // 16) * 16
    logits = parts[0]
    for fellow in range(1, fellows):
        logits = logits + parts[fellow]
    spot = lane_of(logits.shape)
    inside = spot < angles
    highest = jnp.max(jnp.where(inside, logits, -jnp.inf), axis=1, keepdims=True)
    highest = group_of(jnp.broadcast_to(highest, logits.shape), top, jnp.maximum)
    exponent = jnp.where(inside, jnp.exp(logits - highest), 0.0)
    summed = jnp.sum(exponent, axis=1, keepdims=True)
    summed = group_of(jnp.broadcast_to(summed, logits.shape), top, jnp.add)
    post = (exponent / summed).astype(BF16).astype(F32)
    lo = jnp.where(inside, post, roll(post, LANES - angles))
    hi = jnp.where((spot >= cut) & inside, roll(post, cut), roll(post, cut - angles))
    ext_lo[...] = lo.reshape(ext_lo.shape)
    ext_hi[...] = hi.reshape(ext_hi.shape)
    acc[...] = jnp.zeros_like(acc)

    def pair(m):
        lo_rows = ext_lo[m]
        hi_rows = ext_hi[m]
        for k in range(2):
            i = 2 * m + k
            turned = []
            for j in range(top):
                e = k * top + j
                first = pltpu.roll(
                    jnp.broadcast_to(lo_rows[e : e + 1], (8, LANES)), 0, 1, stride=1, stride_axis=0
                )
                second = pltpu.roll(
                    jnp.broadcast_to(hi_rows[e : e + 1], (8, LANES)), 0, 1, stride=1, stride_axis=0
                )
                for tile in range(tiles):
                    if 8 * tile < cut:
                        turned.append(roll(first, 8 * tile) if tile else first)
                    else:
                        shift = 8 * tile - cut
                        turned.append(roll(second, shift) if shift else second)
                for tile in range(tiles, tall_rows // 8):
                    turned.append(second)
            circle = jnp.concatenate(turned, axis=0).astype(BF16)
            grid = jnp.dot(circle, weights_ref[i], preferred_element_type=F32)
            spots = [place_ref[rows_ref[i, j]] for j in range(top)]
            held = [acc[spot] for spot in spots]
            for j in range(top):
                acc[spots[j]] = held[j] + grid[j * tall_rows : j * tall_rows + angles]

    def some(b, carry):
        for m in range(batch // 2):
            pair(b * (batch // 2) + m)
        return carry

    batch = 8
    lax.fori_loop(0, ext_lo.shape[0] // (batch // 2), some, 0)
    lane = lane_of((angles, LANES))

    def pack(owner, carry):
        nums = [None] * num_packs
        dens = [None] * -(-slots // per_den)
        for t in range(per_owner):
            value = acc[owner * per_owner + t]
            g, u = t % per_pack, t // per_pack
            num = roll(value, width * g)
            nums[u] = num if g == 0 else jnp.where(lane >= width * g, num, nums[u])
            h, v = t % per_den, t // per_den
            den = roll(value, half * h - width)
            dens[v] = den if h == 0 else jnp.where(lane >= half * h, den, dens[v])
        for u, value in enumerate(nums + dens):
            out_ref[owner, u] = value.astype(BF16)
        return carry

    lax.fori_loop(0, owners, pack, 0)


def gather_kernel(axis, size, half, slots, x_ref, out_ref, landed, send, recv):
    me = lax.axis_index(axis)
    greet(((axis, size),))
    copies = []
    for step in range(1, size):
        peer = lax.rem(me + step, size)
        copies.append(
            pltpu.make_async_remote_copy(
                src_ref=x_ref.at[peer],
                dst_ref=landed.at[step - 1],
                send_sem=send.at[step],
                recv_sem=recv.at[step],
                device_id={axis: peer},
                device_id_type=MESH,
            )
        )
    for copy in copies:
        copy.start()
    total = x_ref[me].astype(F32)
    for step in range(1, size):
        copies[step - 1].wait_recv()
        total = total + landed[step - 1].astype(F32)
    width = 2 * half
    per_pack = LANES // width
    num_packs = slots // per_pack
    target = lax.broadcasted_iota(jnp.int32, (LANES, LANES), 0)
    source = lax.broadcasted_iota(jnp.int32, (LANES, LANES), 1)
    shell = (target % width) // 2
    flip = target - target % width + (target % 2) * half + shell

    def picked(wanted, x):
        return lax.dot_general(
            (source == wanted).astype(F32),
            x,
            (((1,), (1,)), ((), ())),
            precision=lax.Precision.HIGHEST,
            preferred_element_type=F32,
        )

    for u in range(num_packs):
        held = num_packs + (u * per_pack * half) // LANES
        offset = (u * per_pack * half) % LANES
        den = picked(offset + half * (target // width) + shell, total[held])
        out_ref[u] = picked(flip, total[u]) / (den + 1.0)
    for copy in copies:
        copy.wait_send()


def on_device(images, ctf, classes, class_place, references, sigma2):
    shells = sigma2.shape[0]
    angles = ctf.shape[1] // shells
    particles = images.shape[0]
    per_owner = references.shape[0]
    top = classes.shape[1]
    owners = lax.axis_size("cls")
    fellows = lax.axis_size("img")
    my_fellow = lax.axis_index("img")
    half = shells // fellows
    width = 2 * half
    per_pack = LANES // width
    per_den = LANES // half
    slots = -(-per_owner // per_pack) * per_pack
    dims = (fellows, particles, owners, per_owner, slots, top, angles, half)

    num = images.reshape(particles // per_pack, per_pack, fellows, width, angles)
    num = num.transpose(2, 0, 4, 1, 3).reshape(fellows, -1, angles, LANES)
    den = ctf.reshape(particles // per_den, per_den, fellows, half, angles)
    den = den.transpose(2, 0, 4, 1, 3).reshape(fellows, -1, angles, LANES)
    send = jnp.concatenate([num, den], axis=1)
    mine = lax.dynamic_slice_in_dim(references, my_fellow * (width * angles), width * angles, 1)
    mine = jnp.pad(mine, ((0, slots - per_owner), (0, 0)))
    mine = mine.reshape(slots // per_pack, per_pack, width, angles)[..., ::-1]
    mine = mine.transpose(0, 3, 1, 2).reshape(-1, angles, LANES)
    rows = jnp.pad(classes, ((0, 0), (0, LANES - top)))

    packs = send.shape[1]
    everyone = fellows * particles
    tall_rows = -(-angles // 16) * 16
    pairs = everyone // 2
    smem = pl.BlockSpec(memory_space=pltpu.SMEM)
    dma = pltpu.SemaphoreType.DMA
    parts, weights, tall = pl.pallas_call(
        functools.partial(score_kernel, dims),
        out_shape=(
            jax.ShapeDtypeStruct((fellows, everyone * top, LANES), F32),
            jax.ShapeDtypeStruct((everyone, LANES, LANES), BF16),
            jax.ShapeDtypeStruct((fellows, particles, LANES), jnp.int32),
        ),
        in_specs=[smem] + vmem_specs(4),
        out_specs=tuple(vmem_specs(3)),
        scratch_shapes=[
            VMEM((fellows, packs, angles, LANES), BF16),
            VMEM((owners,) + mine.shape, BF16),
            pltpu.SMEM((fellows, particles, LANES), jnp.int32),
            VMEM((owners * per_owner, tall_rows, LANES), BF16),
            VMEM((particles * top, LANES), F32),
            VMEM((particles * top, LANES), F32),
            VMEM((per_pack, LANES, LANES), BF16),
            VMEM((per_den, LANES, LANES), BF16),
            dma((2,)),
            dma((fellows,)),
            dma((fellows,)),
            dma((owners,)),
            dma((owners,)),
            dma((fellows,)),
            dma((fellows,)),
            dma((fellows, fellows)),
            dma((fellows, fellows)),
        ],
        compiler_params=pltpu.CompilerParams(collective_id=0, has_side_effects=True),
    )(class_place, send, mine, rows, sigma2.reshape(1, shells))
    row_list = tall[:, :, :top].reshape(everyone, top)
    sums = pl.pallas_call(
        functools.partial(total_kernel, dims),
        out_shape=jax.ShapeDtypeStruct(
            (owners, slots // per_pack - (-slots // per_den), angles, LANES), BF16
        ),
        in_specs=[smem, smem] + vmem_specs(2),
        out_specs=pl.BlockSpec(memory_space=pltpu.VMEM),
        scratch_shapes=[
            VMEM((owners * per_owner, angles, LANES), F32),
            VMEM((pairs, 2 * top, LANES), F32),
            VMEM((pairs, 2 * top, LANES), F32),
        ],
    )(class_place, row_list, parts, weights)
    share = pl.pallas_call(
        functools.partial(gather_kernel, "cls", owners, half, slots),
        out_shape=jax.ShapeDtypeStruct((slots // per_pack, LANES, angles), F32),
        in_specs=vmem_specs(1),
        out_specs=pl.BlockSpec(memory_space=pltpu.VMEM),
        scratch_shapes=[
            VMEM((owners - 1,) + sums.shape[1:], BF16),
            pltpu.SemaphoreType.DMA((owners,)),
            pltpu.SemaphoreType.DMA((owners,)),
        ],
        compiler_params=pltpu.CompilerParams(collective_id=2, has_side_effects=True),
    )(sums)
    return share.reshape(slots * width, angles)[: per_owner * width].reshape(per_owner, -1)


def solution(mesh):
    in_specs = (
        P(("cls", "img"), None),
        P(("cls", "img"), None),
        P(("cls", "img"), None),
        P(),
        P("cls", None),
        P(),
    )
    out_specs = P("cls", "img")
    return jax.shard_map(
        on_device, mesh=mesh, in_specs=in_specs, out_specs=out_specs, check_vma=False
    )
```

profile of v0, /device:TPU:10, one launch (start us, length us, event | category | flops | bytes accessed | tf_op | source)
XLA Modules:
  0.0 58.6 jit_solution(12613579820624979240)
XLA Ops:
  0.0 0.0 copy-start
  0.0 0.8 %copy.15 = s32[16,4]{1,0:T(8,128)S(1)} copy(s32[16,4]{0,1:T(4,128)} %param.8) | data formatting | bytes 512 | tf_op args[2]
  0.8 0.6 %pad.9.t_ref = s32[16,128]{1,0:T(8,128)} pad(s32[16,4]{1,0:T(8,128)S(1)} %copy.15, s32[]{:T(128)} %constant.2.clone.1), padding=0_0x0_124 | pad | bytes 8452 | tf_op jit(solution)/shard_map/jit(_pad)/pad | solution.py:378
  1.4 0.0 copy-done
  1.4 0.2 reshape.34
  1.6 0.1 rev.3
  1.7 0.7 %copy.16.r_ref = bf16[2,72,128]{2,1,0:T(8,128)(2,1)} copy(bf16[2,72,128]{1,2,0:T(8,128)(2,1)S(1)} %bitcast.16) | data formatting | bytes 73728 | tf_op jit(solution)/shard_map/reshape | solution.py:377
  2.4 1.4 %reshape.32 = bf16[2,8,4,16,72]{4,3,2,1,0:T(8,128)(2,1)S(1)} reshape(bf16[16,4608]{1,0:T(8,128)(2,1)} %param.7) | data formatting | bytes 294912 | tf_op jit(solution)/shard_map/reshape | solution.py:371
  3.9 0.1 copy.14
  4.0 2.1 %reshape.30 = bf16[4,4,4,32,72]{4,3,2,1,0:T(8,128)(2,1)S(1)} reshape(bf16[16,9216]{1,0:T(8,128)(2,1)} %param.6) | data formatting | bytes 589824 | tf_op jit(solution)/shard_map/reshape | solution.py:369
  6.2 0.2 copy.13
  6.4 0.8 %pad_maximum_fusion.w_ref = bf16[4,6,72,128]{3,2,1,0:T(8,128)(2,1)} fusion(bf16[4,2,72,128]{3,2,1,0:T(8,128)(2,1)S(1)} %copy.14, bf16[4,4,72,128]{3,2,1,0:T(8,128)(2,1)S(1)} %copy.13), kind=kLoop, calls=%fused_computation | loop fusion | flops 221184 | bytes 884736 | tf_op jit(solution)/shard_map/concatenate | solution.py:373
  7.3 23.4 %shard_map.64 = (f32[4,256,128]{2,1,0:T(8,128)}, bf16[64,128,128]{2,1,0:T(8,128)(2,1)}, s32[4,16,128]{2,1,0:T(8,128)}) custom-call(s32[56]{0:T(128)} %place_ref.3, bf16[4,6,72,128]{3,2,1,0:T(8,128)(2,1)} %pad_maximum_fusion.w_ref, bf16[2,72,128]{2,1,0:T(8,128)(2,1)} %copy.16.r_ref, s32[16,128]{1,0:T(8,128)} %pad.9.t_ref, f32[1,64]{1,0:T(1,128)} %bitcast.18), custom_call_target="tpu_custom_call" | custom-call | tf_op jit(solution)/shard_map/pallas_call | solution.py:386
  30.6 9.4 %shard_map.65.x_ref = bf16[8,3,72,128]{3,2,1,0:T(8,128)(2,1)} custom-call(s32[56]{0:T(128)} %place_ref.3, s32[64,4]{1,0:T(8,128)} %bitcast.17, f32[4,256,128]{2,1,0:T(8,128)} %get-tuple-element.9.parts, bf16[64,128,128]{2,1,0:T(8,128)(2,1)} %get-tuple-element.10.weights_ref), custom_call_target="tpu_custom_call" | custom-call | tf_op jit(solution)/shard_map/pallas_call | solution.py:417
  40.0 17.0 %shard_map.66 = f32[2,128,72]{2,1,0:T(8,128)} custom-call(bf16[8,3,72,128]{3,2,1,0:T(8,128)(2,1)} %shard_map.65.x_ref), custom_call_target="tpu_custom_call" | custom-call | tf_op jit(solution)/shard_map/pallas_call | solution.py:430
  57.0 0.9 %slice.8 = f32[224,72]{1,0:T(8,128)S(1)} slice(f32[256,72]{1,0:T(8,128)} %bitcast.15), slice={[0:224], [0:72]} | slice | bytes 129024 | tf_op jit(solution)/shard_map/slice | solution.py:442
  57.9 0.8 %reshape.39 = f32[7,2304]{1,0:T(8,128)} reshape(f32[224,72]{1,0:T(8,128)S(1)} %slice.8) | data formatting | bytes 129024 | tf_op jit(solution)/shard_map/reshape | solution.py:442
  (4 shorter events, 0.1 us)
Async XLA Ops:
  0.0 1.4 %copy-start = (bf16[7,9216]{1,0:T(8,128)(2,1)S(1)}, bf16[7,9216]{1,0:T(8,128)(2,1)}, u32[]{:S(2)}) copy-start(bf16[7,9216]{1,0:T(8,128)(2,1)} %param.10) | copy-start | bytes 387076
where the time goes:
time: 58.9 us; the launch traced here: 58.6 us
  Pallas kernels  49.7 us (84%)
  local copies, waits for them, and re-layouts  8.04 us (14%)
  other arithmetic  0.82 us (1%)
    pallas_call x1, Pallas kernels, on_device(): pl.pallas_call(functools.partial(score_kernel, dims), out_shape=(jax.Shap...  23.4 us
    pallas_call x1, Pallas kernels, on_device(): pl.pallas_call(functools.partial(gather_kernel, 'cls', owners, half, slot...  17 us
    pallas_call x1, Pallas kernels, on_device(): pl.pallas_call(functools.partial(total_kernel, dims), out_shape=jax.Shape...  9.38 us
    reshape x2, local copies, waits for them, and re-layouts, on_device(): images.reshape(particles // per_pack, per_pack, fellows, width, angles)  2.16 us
    reshape x2, local copies, waits for them, and re-layouts, on_device(): den = ctf.reshape(particles // per_den, per_den, fellows, half, angles)  1.46 us

commit v1 on v0

v1 whole, which is shorter than its diff:
```python
import functools

import jax
import jax.numpy as jnp
import numpy as np
from jax import lax
from jax.experimental import pallas as pl
from jax.experimental.pallas import tpu as pltpu
from jax.sharding import PartitionSpec as P

MESH = pl.DeviceIdType.MESH
VMEM = pltpu.VMEM
F32 = jnp.float32
BF16 = jnp.bfloat16
LANES = 128
IMAG = 64
LAST = (((1,), (1,)), ((), ()))


def specs(count, space=pltpu.VMEM):
    return [pl.BlockSpec(memory_space=space)] * count


def round_up(x, step):
    return -(-x // step) * step


def waves(angles):
    turns = angles // 2 + 1
    step = 2 * np.pi * np.outer(np.arange(angles), np.arange(turns)) / angles
    cos = np.zeros((LANES, IMAG))
    sin = np.zeros((LANES, IMAG))
    cos[:angles, :turns] = np.cos(step)
    sin[:angles, :turns] = np.sin(step)
    share = np.zeros((IMAG,))
    share[:turns] = 2.0 / angles
    share[0] = 1.0 / angles
    if angles % 2 == 0:
        share[turns - 1] = 1.0 / angles
    back = np.concatenate([cos * share, -sin * share], axis=1)
    return cos, sin, back


def halves(x):
    high = np.asarray(x, dtype=BF16)
    low = np.asarray(x - high.astype(np.float64), dtype=BF16)
    return high, low


def paired(*forms):
    return np.concatenate([part for form in forms for part in halves(form)], axis=1)


def greet(groups):
    barrier = pltpu.get_barrier_semaphore()
    total = 0
    for axis, size in groups:
        me = lax.axis_index(axis)
        for step in range(1, size):
            peer = lax.rem(me + step, size)
            pl.semaphore_signal(barrier, inc=1, device_id={axis: peer}, device_id_type=MESH)
            total += 1
    pl.semaphore_wait(barrier, total)


def remote(src, dst, send, recv, axis, peer):
    return pltpu.make_async_remote_copy(
        src_ref=src,
        dst_ref=dst,
        send_sem=send,
        recv_sem=recv,
        device_id={axis: peer},
        device_id_type=MESH,
    )


def lane_of(shape):
    return lax.broadcasted_iota(jnp.int32, shape, len(shape) - 1)


def roll(x, shift):
    return pltpu.roll(x, shift % LANES, x.ndim - 1)


def piece(tiles, start, count):
    tile, offset = divmod(start, LANES)
    if offset == 0:
        return tiles[tile]
    first = roll(tiles[tile], -offset)
    if offset + count <= LANES:
        return first
    return jnp.where(lane_of(first.shape) < LANES - offset, first, roll(tiles[tile + 1], -offset))


def tiles_of(x):
    return [x[:, begin : begin + LANES].astype(F32) for begin in range(0, x.shape[1], LANES)]


def group_of(x, top, combine):
    row = lax.broadcasted_iota(jnp.int32, x.shape, 0)
    count = x.shape[0]
    step = 1
    while step < top:
        swapped = jnp.where(
            (row // step) % 2 == 0, pltpu.roll(x, count - step, 0), pltpu.roll(x, step, 0)
        )
        x = combine(x, swapped)
        step *= 2
    return x


def score_kernel(
    dims, place_ref, sigma_ref, w_ref, c_ref, r_ref, t_ref, fw_ref, fr_ref, back_ref,
    what, post, tall,
    wall, call, rall, rows_ref, real, imag, parts, landed,
    own_sem, ws, wr, cs, cr, rs, rr, ts, tr, ls, lr, ps, pr,
):
    fellows, particles, owners, per_owner, top, angles, half = dims
    rows = 3 * half
    wide = wall.shape[2]
    thin = call.shape[2]
    entries = particles * top
    my_owner = lax.axis_index("cls")
    my_fellow = lax.axis_index("img")
    greet((("cls", owners), ("img", fellows)))

    def columns(ref, fellow, count):
        return ref.at[:, pl.ds(pl.multiple_of(fellow * count, LANES), count)]

    mine = columns(r_ref, my_fellow, wide)
    row_copies = []
    ref_copies = []
    image_copies = []
    for step in range(1, fellows):
        peer = lax.rem(my_fellow + step, fellows)
        row_copies.append(remote(t_ref, tall.at[my_fellow], ts.at[step], tr.at[step], "img", peer))
        image_copies.append(
            remote(
                columns(c_ref, peer, thin), call.at[my_fellow], cs.at[step], cr.at[step], "img", peer
            )
        )
        image_copies.append(
            remote(
                columns(w_ref, peer, wide), wall.at[my_fellow], ws.at[step], wr.at[step], "img", peer
            )
        )
    for step in range(1, owners):
        peer = lax.rem(my_owner + step, owners)
        ref_copies.append(remote(mine, rall.at[my_owner], rs.at[step], rr.at[step], "cls", peer))
    for copy in row_copies + ref_copies + image_copies:
        copy.start()
    own_copies = [
        pltpu.make_async_copy(t_ref, tall.at[my_fellow], own_sem.at[0]),
        pltpu.make_async_copy(columns(c_ref, my_fellow, thin), call.at[my_fellow], own_sem.at[1]),
        pltpu.make_async_copy(columns(w_ref, my_fellow, wide), wall.at[my_fellow], own_sem.at[2]),
        pltpu.make_async_copy(mine, rall.at[my_owner], own_sem.at[3]),
    ]
    for copy in own_copies:
        copy.start()

    inverses = [
        1.0 / jnp.full((particles, LANES), sigma_ref[my_fellow * half + s], F32) for s in range(half)
    ]

    flat_real = real.reshape(owners * per_owner * rows, LANES)
    flat_imag = imag.reshape(owners * per_owner * rows, LANES)

    def transform(blocks, table):
        x = jnp.concatenate(blocks, axis=0).astype(BF16)
        return jnp.dot(x, table, preferred_element_type=F32)

    def place(fellow):
        num = tiles_of(wall[fellow])
        den = tiles_of(call[fellow])
        weighted = []
        power = []
        for s in range(half):
            ctf = piece(den, s * angles, angles)
            scale = ctf * inverses[s]
            power.append(ctf * scale)
            for p in range(2):
                weighted.append(piece(num, (2 * s + p) * angles, angles) * scale)
        hat = transform(weighted + power, fw_ref[...])
        hat = hat[:, :LANES] + hat[:, LANES:]
        for row in range(rows):
            what[pl.ds(fellow * (particles * rows) + row, particles, stride=rows)] = hat[
                row * particles : (row + 1) * particles
            ]

    def tabulate(owner):
        ref = tiles_of(rall[owner])
        given = []
        power = []
        for s in range(half):
            pair = [piece(ref, (2 * s + p) * angles, angles) for p in range(2)]
            given += pair
            squares = pair[0] * pair[0] + pair[1] * pair[1]
            power.append(squares.astype(BF16).astype(F32) * -0.5)
        tall_rows = round_up(per_owner, 8)
        blocks = [
            jnp.concatenate([x, jnp.zeros((tall_rows - per_owner, LANES), F32)], axis=0)
            for x in given + power
        ]
        hat = transform(blocks, fr_ref[...])
        for row in range(rows):
            at = pl.ds(owner * (per_owner * rows) + row, per_owner, stride=rows)
            block = hat[row * tall_rows : row * tall_rows + per_owner]
            flat_real[at] = block[:, :LANES] + block[:, LANES : 2 * LANES]
            flat_imag[at] = block[:, 2 * LANES : 3 * LANES] + block[:, 3 * LANES :]

    for copy in own_copies:
        copy.wait()
    place(my_fellow)
    tabulate(my_owner)
    for copy in row_copies:
        copy.wait_recv()
    to_smem = pltpu.make_async_copy(tall, rows_ref, own_sem.at[4])
    to_smem.start()
    for step in range(1, max(owners, fellows)):
        if step < fellows:
            image_copies[2 * step - 2].wait_recv()
            image_copies[2 * step - 1].wait_recv()
            place(lax.rem(my_fellow + fellows - step, fellows))
        if step < owners:
            ref_copies[step - 1].wait_recv()
            tabulate(lax.rem(my_owner + owners - step, owners))
    to_smem.wait()

    batch = 4

    def score(fellow):
        def some(b, carry):
            sums = []
            for k in range(batch):
                i = b * batch + k
                base = pl.multiple_of((fellow * particles + i) * rows, 8)
                held = what[pl.ds(base, rows)]
                for j in range(top):
                    row = place_ref[rows_ref[fellow, j, i]]
                    first = held * real[row]
                    second = held * imag[row]
                    first = jnp.sum(first.reshape(rows // 8, 8, LANES), axis=0)
                    second = jnp.sum(second.reshape(rows // 8, 8, LANES), axis=0)
                    sums.append(jnp.sum(first + roll(second, IMAG), axis=0, keepdims=True))
            count = batch * top
            parts[fellow, pl.ds(pl.multiple_of(b * count, count), count)] = jnp.concatenate(
                sums, axis=0
            )
            return carry

        lax.fori_loop(0, particles // batch, some, 0)

    part_copies = []
    for step in range(1, fellows):
        peer = lax.rem(my_fellow + fellows - step, fellows)
        score(peer)
        copy = remote(
            parts.at[peer], landed.at[step - 1], ls.at[step], lr.at[step], "img", peer
        )
        copy.start()
        part_copies.append(copy)
    score(my_fellow)
    total = parts[my_fellow]
    for step in range(1, fellows):
        part_copies[step - 1].wait_recv()
        total = total + landed[step - 1]
    logits = jnp.dot(
        total, back_ref[...], precision=lax.Precision.HIGHEST, preferred_element_type=F32
    )
    inside = lane_of(logits.shape) < angles
    highest = jnp.max(jnp.where(inside, logits, -jnp.inf), axis=1, keepdims=True)
    highest = group_of(jnp.broadcast_to(highest, logits.shape), top, jnp.maximum)
    exponent = jnp.where(inside, jnp.exp(logits - highest), 0.0)
    summed = jnp.sum(exponent, axis=1, keepdims=True)
    summed = group_of(jnp.broadcast_to(summed, logits.shape), top, jnp.add)
    post[my_fellow] = (exponent / summed).astype(BF16)
    post_copies = []
    for step in range(1, fellows):
        peer = lax.rem(my_fellow + step, fellows)
        at = post.at[my_fellow]
        copy = remote(at, at, ps.at[step], pr.at[step], "img", peer)
        copy.start()
        post_copies.append(copy)
    for copy in row_copies + ref_copies + image_copies + part_copies:
        copy.wait_send()
    for copy in post_copies:
        copy.wait()


def total_kernel(dims, place_ref, rows_ref, what, post, fp_ref, acc, real, imag):
    fellows, particles, owners, per_owner, top, angles, half = dims
    rows = 3 * half
    hat = jnp.dot(post[...].reshape(-1, LANES), fp_ref[...], preferred_element_type=F32)
    real[...] = hat[:, :LANES] + hat[:, LANES : 2 * LANES]
    imag[...] = hat[:, 2 * LANES : 3 * LANES] + hat[:, 3 * LANES :]
    acc[...] = jnp.zeros_like(acc)
    batch = 4

    def one(fellow, i):
        at = fellow * particles + i
        held = what[pl.ds(pl.multiple_of(at * rows, 8), rows)]
        swapped = roll(held, IMAG)
        spots = [
            pl.ds(pl.multiple_of(place_ref[rows_ref[fellow, j, i]] * rows, 8), rows)
            for j in range(top)
        ]
        before = [acc[spot] for spot in spots]
        for j in range(top):
            e = at * top + j
            acc[spots[j]] = before[j] + held * real[pl.ds(e, 1)] + swapped * imag[pl.ds(e, 1)]

    def some(b, carry):
        for k in range(batch):
            one(b // (particles // batch), lax.rem(b, particles // batch) * batch + k)
        return carry

    lax.fori_loop(0, fellows * particles // batch, some, 0)


def gather_kernel(dims, acc, high_ref, low_ref, out_ref, outbox, landed, flat, send, recv):
    fellows, particles, owners, per_owner, top, angles, half = dims
    rows = 3 * half
    lanes = outbox.shape[2]
    me = lax.axis_index("cls")
    greet((("cls", owners),))

    def sums(owner):
        x = acc[pl.ds(pl.multiple_of(owner * (per_owner * rows), 8), lanes)]
        high = x.astype(BF16)
        low = (x - high.astype(F32)).astype(BF16)

        def turned(a, b):
            return lax.dot_general(a, b, LAST, preferred_element_type=F32)

        return turned(high_ref[...], high) + (
            turned(high_ref[...], low) + turned(low_ref[...], high)
        )

    copies = []
    for step in range(1, owners):
        peer = lax.rem(me + step, owners)
        outbox[peer] = sums(peer)[:angles].astype(BF16)
        copy = remote(
            outbox.at[peer], landed.at[step - 1], send.at[step], recv.at[step], "cls", peer
        )
        copy.start()
        copies.append(copy)
    total = sums(me)[:angles]
    for step in range(1, owners):
        copies[step - 1].wait_recv()
        total = total + landed[step - 1].astype(F32)
    total = jnp.concatenate([total, jnp.zeros((LANES - angles, lanes), F32)], axis=0)
    for begin in range(0, lanes, LANES):
        flat[begin : begin + LANES] = total[:, begin : begin + LANES].T
    count = out_ref.shape[1] // LANES
    tiles = [jnp.zeros((per_owner, LANES), F32) for _ in range(count)]
    lane = lane_of((per_owner, LANES))
    for s in range(half):
        den = flat[pl.ds(2 * half + s, per_owner, stride=rows)] + 1.0
        for p in range(2):
            new = flat[pl.ds(2 * s + p, per_owner, stride=rows)] / den
            tile, offset = divmod((2 * s + p) * angles, LANES)
            new = roll(new, offset) if offset else new
            within = (lane >= offset) & (lane < offset + angles)
            tiles[tile] = jnp.where(within, new, tiles[tile])
            if offset + angles > LANES:
                tiles[tile + 1] = jnp.where(lane < offset + angles - LANES, new, tiles[tile + 1])
    for tile, value in enumerate(tiles):
        out_ref[:, tile * LANES : (tile + 1) * LANES] = value
    for copy in copies:
        copy.wait_send()


def spaced(x, fellows):
    count = x.shape[1] // fellows
    wanted = round_up(count, LANES)
    if wanted == count:
        return x, count
    x = jnp.pad(x.reshape(x.shape[0], fellows, count), ((0, 0), (0, 0), (0, wanted - count)))
    return x.reshape(x.shape[0], fellows * wanted), wanted


def on_device(images, ctf, classes, class_place, references, sigma2):
    shells = sigma2.shape[0]
    angles = ctf.shape[1] // shells
    particles = images.shape[0]
    per_owner = references.shape[0]
    top = classes.shape[1]
    owners = lax.axis_size("cls")
    fellows = lax.axis_size("img")
    half = shells // fellows
    rows = 3 * half
    dims = (fellows, particles, owners, per_owner, top, angles, half)
    everyone = fellows * particles
    total = owners * per_owner
    lanes = round_up(per_owner * rows, LANES)
    acc_rows = round_up((total - per_owner) * rows + lanes, 8)

    images, wide = spaced(images, fellows)
    ctf, thin = spaced(ctf, fellows)
    references, _ = spaced(references, fellows)

    cos, sin, back = waves(angles)
    both = np.concatenate([cos, cos], axis=1)
    forward = jnp.asarray(paired(np.concatenate([cos, -sin], axis=1)))
    of_refs = jnp.asarray(paired(both, np.concatenate([sin, -sin], axis=1)))
    of_post = jnp.asarray(paired(both, np.concatenate([-sin, sin], axis=1)))
    back_high, back_low = halves(back[: round_up(angles, 16)])
    smem = pl.BlockSpec(memory_space=pltpu.SMEM)
    dma = pltpu.SemaphoreType.DMA
    what, post, tall = pl.pallas_call(
        functools.partial(score_kernel, dims),
        out_shape=(
            jax.ShapeDtypeStruct((everyone * rows, LANES), F32),
            jax.ShapeDtypeStruct((fellows, particles * top, LANES), BF16),
            jax.ShapeDtypeStruct((fellows, top, particles), jnp.int32),
        ),
        in_specs=[smem, smem] + specs(4, pl.ANY) + specs(3),
        out_specs=tuple(specs(3)),
        scratch_shapes=[
            VMEM((fellows, particles, wide), BF16),
            VMEM((fellows, particles, thin), BF16),
            VMEM((owners, per_owner, wide), BF16),
            pltpu.SMEM((fellows, top, particles), jnp.int32),
            VMEM((total, rows, LANES), F32),
            VMEM((total, rows, LANES), F32),
            VMEM((fellows, particles * top, LANES), F32),
            VMEM((fellows - 1, particles * top, LANES), F32),
            dma((5,)),
            dma((fellows,)),
            dma((fellows,)),
            dma((fellows,)),
            dma((fellows,)),
            dma((owners,)),
            dma((owners,)),
            dma((fellows,)),
            dma((fellows,)),
            dma((fellows,)),
            dma((fellows,)),
            dma((fellows,)),
            dma((fellows,)),
        ],
        compiler_params=pltpu.CompilerParams(collective_id=0, has_side_effects=True),
    )(
        class_place, sigma2, images, ctf, references, classes.T,
        forward, of_refs, jnp.asarray(back.T, F32),
    )
    acc = pl.pallas_call(
        functools.partial(total_kernel, dims),
        out_shape=jax.ShapeDtypeStruct((acc_rows, LANES), F32),
        in_specs=[smem, smem] + specs(3),
        out_specs=specs(1)[0],
        scratch_shapes=[VMEM((everyone * top, LANES), F32)] * 2,
    )(class_place, tall, what, post, of_post)
    return pl.pallas_call(
        functools.partial(gather_kernel, dims),
        out_shape=jax.ShapeDtypeStruct((per_owner, 2 * half * angles), F32),
        in_specs=specs(3),
        out_specs=specs(1)[0],
        scratch_shapes=[
            VMEM((owners, angles, lanes), BF16),
            VMEM((owners - 1, angles, lanes), BF16),
            VMEM((lanes, LANES), F32),
            dma((owners,)),
            dma((owners,)),
        ],
        compiler_params=pltpu.CompilerParams(collective_id=2, has_side_effects=True),
    )(acc, jnp.asarray(back_high), jnp.asarray(back_low))


def solution(mesh):
    in_specs = (
        P(("cls", "img"), None),
        P(("cls", "img"), None),
        P(("cls", "img"), None),
        P(),
        P("cls", None),
        P(),
    )
    out_specs = P("cls", "img")
    return jax.shard_map(
        on_device, mesh=mesh, in_specs=in_specs, out_specs=out_specs, check_vma=False
    )
```

time: 58.9 us -> 46 us (0.78)
  local copies, waits for them, and re-layouts: 8.04 us -> 1.52 us
  Pallas kernels: 49.7 us -> 44.1 us
  other arithmetic: 0.82 us -> 0 us
    reshape x9 -> x0, local copies, waits for them, and re-layouts: 5.61 us -> none  [the longest x2 2.16 us: on_device(): images.reshape(particles // per_pack, per_pack, fellows, width, angles)]
    pallas_call x1, Pallas kernels: 9.38 us -> 4.9 us  [on_device(): pl.pallas_call(functools.partial(total_kernel, dims), out_shape=jax.Shape...]
    pallas_call x1, Pallas kernels: 23.4 us -> 21.7 us  [on_device(): pl.pallas_call(functools.partial(score_kernel, dims), out_shape=(jax.Shap...]
    slice x1 -> x0, local copies, waits for them, and re-layouts: 0.91 us -> none  [on_device(): share.reshape(slots * width, angles)[:per_owner * width]]
    concatenate x1 -> x0, other arithmetic: 0.82 us -> none  [on_device(): send = jnp.concatenate([num, den], axis=1)]
    unnamed x3 -> x1, local copies, waits for them, and re-layouts: 0.8 us -> 1.52 us
    pad x2 -> x0, local copies, waits for them, and re-layouts: 0.61 us -> none  [the longest x1 0.6 us: on_device(): rows = jnp.pad(classes, ((0, 0), (0, LANES - top)))]
where the time goes in v1:
time: 46 us; the launch traced here: 45.7 us
  Pallas kernels  44.1 us (96%)
  local copies, waits for them, and re-layouts  1.52 us (3%)
    pallas_call x1, Pallas kernels, on_device(): pl.pallas_call(functools.partial(score_kernel, dims), out_shape=(jax.Shap...  21.7 us
    pallas_call x1, Pallas kernels, on_device(): pl.pallas_call(functools.partial(gather_kernel, dims), out_shape=jax.Shap...  17.5 us
    pallas_call x1, Pallas kernels, on_device(): pl.pallas_call(functools.partial(total_kernel, dims), out_shape=jax.Shape...  4.9 us
    unnamed x1, local copies, waits for them, and re-layouts  1.52 us

profile of v1, /device:TPU:10, one launch (start us, length us, event | category | flops | bytes accessed | tf_op | source)
XLA Modules:
  0.0 45.7 jit_solution(10801751752140175509)
XLA Ops:
  0.0 21.7 %shard_map.118 = (f32[3072,128]{1,0:T(8,128)}, bf16[4,64,128]{2,1,0:T(8,128)(2,1)}, s32[4,4,16]{2,1,0:T(4,128)}) custom-call(s32[56]{0:T(128)} %place_ref.3, f32[64]{0:T(128)} %sigma_ref.1, bf16[16,9216]{1,0:T(8,128)(2,1)} %w_ref.1, bf16[16,4608]{1,0:T(8,128)(2,1)} %c_ref.1, bf16[7,9216]{1,0:T(8,128)(2,1)} %r_ref.1, s32[4,16]{1,0:T(4,128)} %bitcast.1, ...), custom_call_target="tpu_custom_call" | custom-call | tf_op jit(solution)/shard_map/pallas_call | solution.py:411
  21.7 4.9 %shard_map.119.acc = f32[2736,128]{1,0:T(8,128)} custom-call(s32[56]{0:T(128)} %place_ref.3, s32[4,4,16]{2,1,0:T(4,128)} %get-tuple-element.8.rows_ref, f32[3072,128]{1,0:T(8,128)} %get-tuple-element.9.what, bf16[4,64,128]{2,1,0:T(8,128)(2,1)} %get-tuple-element.10.post, bf16[128,512]{1,0:T(8,128)(2,1)} %constant.14.clone.fp_ref), custom_call_target="tpu_custom_call" | custom-call | tf_op jit(solution)/shard_map/pallas_call | solution.py:448
  26.6 17.5 %shard_map.120 = f32[7,2304]{1,0:T(8,128)} custom-call(f32[2736,128]{1,0:T(8,128)} %shard_map.119.acc, bf16[80,128]{1,0:T(8,128)(2,1)} %constant.16.clone.high_ref, bf16[80,128]{1,0:T(8,128)(2,1)} %constant.17.clone.low_ref), custom_call_target="tpu_custom_call" | custom-call | tf_op jit(solution)/shard_map/pallas_call | solution.py:455
  44.2 1.5 %copy.14 = f32[7,2304]{1,0:T(8,128)} copy(f32[7,2304]{1,0:T(8,128)} %shard_map.120) | data formatting | bytes 129024

commit v2 on v1

--- a/solution.py
+++ b/solution.py
@@ -14,6 +14,8 @@
 BF16 = jnp.bfloat16
 LANES = 128
 IMAG = 64
+LIMIT = 20 * 2**20
+WIDE = 61500000
 LAST = (((1,), (1,)), ((), ()))
 
 
@@ -51,7 +53,7 @@
     return np.concatenate([part for form in forms for part in halves(form)], axis=1)
 
 
-def greet(groups):
+def hail(groups):
     barrier = pltpu.get_barrier_semaphore()
     total = 0
     for axis, size in groups:
@@ -60,7 +62,7 @@
             peer = lax.rem(me + step, size)
             pl.semaphore_signal(barrier, inc=1, device_id={axis: peer}, device_id_type=MESH)
             total += 1
-    pl.semaphore_wait(barrier, total)
+    return lambda: pl.semaphore_wait(barrier, total)
 
 
 def remote(src, dst, send, recv, axis, peer):
@@ -110,8 +112,9 @@
 
 
 def score_kernel(
-    dims, place_ref, sigma_ref, w_ref, c_ref, r_ref, t_ref, fw_ref, fr_ref, back_ref,
-    what, post, tall,
+    dims, place_hbm, sigma_hbm, w_ref, c_ref, r_ref, t_ref, fw_hbm, fr_hbm, fp_hbm, back_hbm,
+    what, post_real, post_imag, tall, place_out,
+    place_ref, sigma_ref, fw_ref, fr_ref, fp_ref, back_ref, post,
     wall, call, rall, rows_ref, real, imag, parts, landed,
     own_sem, ws, wr, cs, cr, rs, rr, ts, tr, ls, lr, ps, pr,
 ):
@@ -122,7 +125,7 @@
     entries = particles * top
     my_owner = lax.axis_index("cls")
     my_fellow = lax.axis_index("img")
-    greet((("cls", owners), ("img", fellows)))
+    arrive = hail((("cls", owners), ("img", fellows)))
 
     def columns(ref, fellow, count):
         return ref.at[:, pl.ds(pl.multiple_of(fellow * count, LANES), count)]
@@ -147,9 +150,14 @@
     for step in range(1, owners):
         peer = lax.rem(my_owner + step, owners)
         ref_copies.append(remote(mine, rall.at[my_owner], rs.at[step], rr.at[step], "cls", peer))
-    for copy in row_copies + ref_copies + image_copies:
-        copy.start()
     own_copies = [
+        pltpu.make_async_copy(place_hbm, place_ref, own_sem.at[5]),
+        pltpu.make_async_copy(place_hbm, place_out, own_sem.at[6]),
+        pltpu.make_async_copy(sigma_hbm, sigma_ref, own_sem.at[7]),
+        pltpu.make_async_copy(fw_hbm, fw_ref, own_sem.at[8]),
+        pltpu.make_async_copy(fr_hbm, fr_ref, own_sem.at[9]),
+        pltpu.make_async_copy(fp_hbm, fp_ref, own_sem.at[10]),
+        pltpu.make_async_copy(back_hbm, back_ref, own_sem.at[11]),
         pltpu.make_async_copy(t_ref, tall.at[my_fellow], own_sem.at[0]),
         pltpu.make_async_copy(columns(c_ref, my_fellow, thin), call.at[my_fellow], own_sem.at[1]),
         pltpu.make_async_copy(columns(w_ref, my_fellow, wide), wall.at[my_fellow], own_sem.at[2]),
@@ -157,6 +165,11 @@
     ]
     for copy in own_copies:
         copy.start()
+    arrive()
+    for copy in row_copies + ref_copies + image_copies:
+        copy.start()
+    for copy in own_copies:
+        copy.wait()
 
     inverses = [
         1.0 / jnp.full((particles, LANES), sigma_ref[my_fellow * half + s], F32) for s in range(half)
@@ -208,8 +221,6 @@
             flat_real[at] = block[:, :LANES] + block[:, LANES : 2 * LANES]
             flat_imag[at] = block[:, 2 * LANES : 3 * LANES] + block[:, 3 * LANES :]
 
-    for copy in own_copies:
-        copy.wait()
     place(my_fellow)
     tabulate(my_owner)
     for copy in row_copies:
@@ -285,14 +296,16 @@
         copy.wait_send()
     for copy in post_copies:
         copy.wait()
-
-
-def total_kernel(dims, place_ref, rows_ref, what, post, fp_ref, acc, real, imag):
+    hat = jnp.dot(
+        post[...].reshape(fellows * entries, LANES), fp_ref[...], preferred_element_type=F32
+    )
+    post_real[...] = hat[:, :LANES] + hat[:, LANES : 2 * LANES]
+    post_imag[...] = hat[:, 2 * LANES : 3 * LANES] + hat[:, 3 * LANES :]
+
+
+def total_kernel(dims, place_ref, rows_ref, what, real, imag, acc):
     fellows, particles, owners, per_owner, top, angles, half = dims
     rows = 3 * half
-    hat = jnp.dot(post[...].reshape(-1, LANES), fp_ref[...], preferred_element_type=F32)
-    real[...] = hat[:, :LANES] + hat[:, LANES : 2 * LANES]
-    imag[...] = hat[:, 2 * LANES : 3 * LANES] + hat[:, 3 * LANES :]
     acc[...] = jnp.zeros_like(acc)
     batch = 4
 
@@ -322,7 +335,7 @@
     rows = 3 * half
     lanes = outbox.shape[2]
     me = lax.axis_index("cls")
-    greet((("cls", owners),))
+    arrive = hail((("cls", owners),))
 
     def sums(owner):
         x = acc[pl.ds(pl.multiple_of(owner * (per_owner * rows), 8), lanes)]
@@ -340,11 +353,14 @@
     for step in range(1, owners):
         peer = lax.rem(me + step, owners)
         outbox[peer] = sums(peer)[:angles].astype(BF16)
-        copy = remote(
-            outbox.at[peer], landed.at[step - 1], send.at[step], recv.at[step], "cls", peer
+        copies.append(
+            remote(outbox.at[peer], landed.at[step - 1], send.at[step], recv.at[step], "cls", peer)
         )
-        copy.start()
-        copies.append(copy)
+        if step == 2:
+            arrive()
+            copies[0].start()
+        if step >= 2:
+            copies[-1].start()
     total = sums(me)[:angles]
     for step in range(1, owners):
         copies[step - 1].wait_recv()
@@ -408,16 +424,25 @@
     back_high, back_low = halves(back[: round_up(angles, 16)])
     smem = pl.BlockSpec(memory_space=pltpu.SMEM)
     dma = pltpu.SemaphoreType.DMA
-    what, post, tall = pl.pallas_call(
+    what, real, imag, tall, placed = pl.pallas_call(
         functools.partial(score_kernel, dims),
         out_shape=(
             jax.ShapeDtypeStruct((everyone * rows, LANES), F32),
-            jax.ShapeDtypeStruct((fellows, particles * top, LANES), BF16),
+            jax.ShapeDtypeStruct((everyone * top, LANES), F32),
+            jax.ShapeDtypeStruct((everyone * top, LANES), F32),
             jax.ShapeDtypeStruct((fellows, top, particles), jnp.int32),
+            jax.ShapeDtypeStruct((total,), jnp.int32),
         ),
-        in_specs=[smem, smem] + specs(4, pl.ANY) + specs(3),
-        out_specs=tuple(specs(3)),
+        in_specs=specs(10, pltpu.HBM),
+        out_specs=tuple(specs(5)),
         scratch_shapes=[
+            pltpu.SMEM((total,), jnp.int32),
+            pltpu.SMEM((shells,), F32),
+            VMEM(forward.shape, BF16),
+            VMEM(of_refs.shape, BF16),
+            VMEM(of_post.shape, BF16),
+            VMEM(back.shape, F32),
+            VMEM((fellows, particles * top, LANES), BF16),
             VMEM((fellows, particles, wide), BF16),
             VMEM((fellows, particles, thin), BF16),
             VMEM((owners, per_owner, wide), BF16),
@@ -426,7 +451,7 @@
             VMEM((total, rows, LANES), F32),
             VMEM((fellows, particles * top, LANES), F32),
             VMEM((fellows - 1, particles * top, LANES), F32),
-            dma((5,)),
+            dma((12,)),
             dma((fellows,)),
             dma((fellows,)),
             dma((fellows,)),
@@ -440,18 +465,20 @@
             dma((fellows,)),
             dma((fellows,)),
         ],
-        compiler_params=pltpu.CompilerParams(collective_id=0, has_side_effects=True),
+        compiler_params=pltpu.CompilerParams(
+            collective_id=0, has_side_effects=True, vmem_limit_bytes=WIDE
+        ),
     )(
         class_place, sigma2, images, ctf, references, classes.T,
-        forward, of_refs, jnp.asarray(back.T, F32),
+        forward, of_refs, of_post, jnp.asarray(back.T, F32),
     )
     acc = pl.pallas_call(
         functools.partial(total_kernel, dims),
         out_shape=jax.ShapeDtypeStruct((acc_rows, LANES), F32),
         in_specs=[smem, smem] + specs(3),
         out_specs=specs(1)[0],
-        scratch_shapes=[VMEM((everyone * top, LANES), F32)] * 2,
-    )(class_place, tall, what, post, of_post)
+        compiler_params=pltpu.CompilerParams(vmem_limit_bytes=WIDE),
+    )(placed, tall, what, real, imag)
     return pl.pallas_call(
         functools.partial(gather_kernel, dims),
         out_shape=jax.ShapeDtypeStruct((per_owner, 2 * half * angles), F32),
@@ -464,7 +491,9 @@
             dma((owners,)),
             dma((owners,)),
         ],
-        compiler_params=pltpu.CompilerParams(collective_id=2, has_side_effects=True),
+        compiler_params=pltpu.CompilerParams(
+            collective_id=2, has_side_effects=True, vmem_limit_bytes=LIMIT
+        ),
     )(acc, jnp.asarray(back_high), jnp.asarray(back_low))
 
 

time: 46 us -> 43.1 us (0.937)
  Pallas kernels: 44.1 us -> 40.7 us
  local copies, waits for them, and re-layouts: 1.52 us -> 1.99 us
    pallas_call x1, Pallas kernels: 17.5 us -> 15 us  [on_device(): pl.pallas_call(functools.partial(gather_kernel, dims), out_shape=jax.Shap...]
    pallas_call x1, Pallas kernels: 21.7 us -> 20.8 us  [on_device(): pl.pallas_call(functools.partial(score_kernel, dims), out_shape=(jax.Shap...]
    unnamed x1 -> x7, local copies, waits for them, and re-layouts: 1.52 us -> 1.99 us
where the time goes in v2:
time: 43.1 us; the launch traced here: 42.7 us
  Pallas kernels  40.7 us (94%)
  local copies, waits for them, and re-layouts  1.99 us (5%)
    pallas_call x1, Pallas kernels, on_device(): pl.pallas_call(functools.partial(score_kernel, dims), out_shape=(jax.Shap...  20.8 us
    pallas_call x1, Pallas kernels, on_device(): pl.pallas_call(functools.partial(gather_kernel, dims), out_shape=jax.Shap...  15 us
    pallas_call x1, Pallas kernels, on_device(): pl.pallas_call(functools.partial(total_kernel, dims), out_shape=jax.Shape...  4.83 us
    unnamed x7, local copies, waits for them, and re-layouts  1.99 us

profile of v2, /device:TPU:10, one launch (start us, length us, event | category | flops | bytes accessed | tf_op | source)
XLA Modules:
  0.0 42.7 jit_solution(7146105962729689351)
XLA Ops:
  0.0 20.8 %shard_map.118 = (f32[3072,128]{1,0:T(8,128)}, f32[256,128]{1,0:T(8,128)}, f32[256,128]{1,0:T(8,128)}, s32[4,4,16]{2,1,0:T(4,128)}, s32[56]{0:T(128)}) custom-call(s32[56]{0:T(128)} %place_hbm.1, f32[64]{0:T(128)} %sigma_hbm.1, bf16[16,9216]{1,0:T(8,128)(2,1)} %w_ref.1, bf16[16,4608]{1,0:T(8,128)(2,1)} %c_ref.1, bf16[7,9216]{1,0:T(8,128)(2,1)} %r_ref.1, ...), custom_call_target="tpu_custom_call" | custom-call | tf_op jit(solution)/shard_map/pallas_call | solution.py:427
  20.8 0.0 copy-start.1
  20.9 0.0 copy-start.2
  20.9 4.8 %shard_map.119.acc = f32[2736,128]{1,0:T(8,128)} custom-call(s32[56]{0:T(128)} %get-tuple-element.10.place_ref, s32[4,4,16]{2,1,0:T(4,128)} %get-tuple-element.11.rows_ref, f32[3072,128]{1,0:T(8,128)} %get-tuple-element.12.what, f32[256,128]{1,0:T(8,128)} %get-tuple-element.13.real, f32[256,128]{1,0:T(8,128)} %get-tuple-element.14.imag), custom_call_target="tpu_custom_call" | custom-call | tf_op jit(solution)/shard_map/pallas_call | solution.py:475
  25.7 0.0 copy-done.1
  25.7 0.0 copy-done.2
  25.7 0.0 copy-start
  25.7 1.3 %copy-done = f32[2736,128]{1,0:T(8,128)S(1)} copy-done((f32[2736,128]{1,0:T(8,128)S(1)}, f32[2736,128]{1,0:T(8,128)}, u32[]{:S(2)}) %copy-start) | copy-done | bytes 1400856
  27.1 15.0 %shard_map.120 = f32[7,2304]{1,0:T(8,128)S(1)} custom-call(f32[2736,128]{1,0:T(8,128)S(1)} %copy-done, bf16[80,128]{1,0:T(8,128)(2,1)S(1)} %copy-done.2, bf16[80,128]{1,0:T(8,128)(2,1)S(1)} %copy-done.1), custom_call_target="tpu_custom_call" | custom-call | tf_op jit(solution)/shard_map/pallas_call | solution.py:482
  42.1 0.6 %copy.14 = f32[7,2304]{1,0:T(8,128)} copy(f32[7,2304]{1,0:T(8,128)S(1)} %shard_map.120) | data formatting | bytes 129024
Async XLA Ops:
  20.8 4.9 %copy-start.1 = (bf16[80,128]{1,0:T(8,128)(2,1)S(1)}, bf16[80,128]{1,0:T(8,128)(2,1)}, u32[]{:S(2)}) copy-start(bf16[80,128]{1,0:T(8,128)(2,1)} %constant.17.clone.low_ref) | copy-start | bytes 61444
  20.9 4.8 %copy-start.2 = (bf16[80,128]{1,0:T(8,128)(2,1)S(1)}, bf16[80,128]{1,0:T(8,128)(2,1)}, u32[]{:S(2)}) copy-start(bf16[80,128]{1,0:T(8,128)(2,1)} %constant.16.clone.high_ref) | copy-start | bytes 61444
  25.7 1.3 %copy-start = (f32[2736,128]{1,0:T(8,128)S(1)}, f32[2736,128]{1,0:T(8,128)}, u32[]{:S(2)}) copy-start(f32[2736,128]{1,0:T(8,128)} %shard_map.119.acc) | copy-start | bytes 4202500
